TPU v7x, 128 devices: a whole 4x4x4 slice. The times are simulated.
128 devices in a mesh: dp: 16 (over x, z), tensor: 8 (over y, core).
Axes of the slice: x: 4, y: 4, z: 4, core: 2. Of those that a mesh axis runs over, the one named last changes fastest.
Arguments:
- attn_out: bfloat16 [8192, 8192], P('dp', 'tensor'), may hold values from -6 to 6
- frozen_weight: bfloat16 [8192, 8192], P('tensor', 'dp'), may hold values from -0.0625 to 0.0625
- vector_bank: float32 [256, 256], replicated, may hold values from -0.18 to 0.18
- logits_a: float32 [16, 32, 2], P(None, 'tensor'), may hold values from -2 to 2
- index_a: int32 [16, 32, 2], P(None, 'tensor'), may hold values from 0 to 255, all different within a row
- logits_b: float32 [16, 32, 2], P(None, 'tensor'), may hold values from -2 to 2
- index_b: int32 [16, 32, 2], P(None, 'tensor'), may hold values from 0 to 255, all different within a row
- out_grad: bfloat16 [8192, 8192], P('dp'), may hold values from -6 to 6
Outputs:
- layer_out: bfloat16 [8192, 8192], P('dp', 'tensor')
- attn_grad: bfloat16 [8192, 8192], P('dp', 'tensor')
- bank_grad: float32 [256, 256], replicated
- logits_a_grad: float32 [16, 32, 2], P(None, 'tensor')
- logits_b_grad: float32 [16, 32, 2], P(None, 'tensor')
Inputs may be any that keep to these rules, and one draw needn't show every extreme that they name: `index_a`: the 2 entries of one sub-vector differ. `index_b`: the 2 entries of one sub-vector differ.
All inputs are finite; a program needn't handle non-finite values.
Results may differ from a plain program's by a relative error of at most 0.014.
Values may be sent and summed in bfloat16 or wider, within the bound.
No kernel may reach another device: no remote copies, remote signals or barrier semaphores. Data moves between devices by JAX's collectives and lax.ppermute only.
A program may use at most 128 MiB of HBM per device.

v0:
```python
import jax
import jax.numpy as jnp
from jax import lax
from jax.sharding import PartitionSpec as P

adapter_scale = 2.0


def from_everyone(x, axis):
    copies = jnp.broadcast_to(x, (lax.axis_size(axis), *x.shape))
    return lax.all_to_all(copies, axis, split_axis=0, concat_axis=0, tiled=True)


def over_copies(x, axis):
    everything = from_everyone(x, axis)
    return jnp.sum(everything, axis=0)


def packed_total(arrays, axis):
    ends = [0]
    for a in arrays:
        ends.append(ends[-1] + a.size)
    running = over_copies(jnp.concatenate([a.ravel() for a in arrays]), axis)
    return tuple((running[b:e].reshape(a.shape) for a, b, e in zip(arrays, ends, ends[1:])))


def gathered_total(x, axis):
    parts = lax.all_gather(x, axis)
    return parts.sum(axis=0)


def compose(logits, indices, vector_bank):
    weights = jax.nn.sigmoid(logits - logits[..., ::-1])
    levels = jnp.arange(vector_bank.shape[0], dtype=jnp.int32)
    picked = (indices[..., None] == levels).astype(jnp.float32)
    mixing = jnp.sum(picked * weights[..., None], axis=2)
    blocks = jnp.einsum("rjb,bc->rjc", mixing, vector_bank, precision=lax.Precision.HIGHEST)
    return (weights, picked, mixing, blocks.reshape(blocks.shape[0], -1))


def compose_back(grad_rows, weights, picked, mixing, vector_bank):
    blocks = grad_rows.reshape(mixing.shape[0], mixing.shape[1], -1)
    bank_part = jnp.einsum("rjb,rjc->bc", mixing, blocks, precision=lax.Precision.HIGHEST)
    projected = jnp.einsum("rjc,bc->rjb", blocks, vector_bank, precision=lax.Precision.HIGHEST)
    dots = jnp.sum(picked * projected[:, :, None, :], axis=3)
    logit_grad = weights * (dots - jnp.sum(weights * dots, axis=2, keepdims=True))
    return (bank_part, logit_grad)


def local(attn_out, frozen_weight, vector_bank, logits_a, index_a, logits_b, index_b, out_grad):
    weights_a, picked_a, mixing_a, rows_a = compose(logits_a, index_a, vector_bank)
    weights_b, picked_b, mixing_b, rows_b = compose(logits_b, index_b, vector_bank)
    down_a = rows_a.astype(jnp.bfloat16)
    up_b = rows_b.astype(jnp.bfloat16)
    own_width = up_b.shape[1]
    grad_cols = lax.dynamic_slice_in_dim(
        out_grad, lax.axis_index("tensor") * own_width, own_width, 1
    )
    low_part = jnp.dot(attn_out, down_a.T, preferred_element_type=jnp.float32)
    back_part = jnp.dot(grad_cols, up_b.T, preferred_element_type=jnp.float32)
    low_total, back_total = packed_total((low_part, back_part), "tensor")
    low_bf = low_total.astype(jnp.bfloat16)
    gathered = lax.all_gather(frozen_weight, "dp", axis=1, tiled=True)
    partial_value = jnp.dot(attn_out, gathered, preferred_element_type=jnp.float32).astype(
        jnp.bfloat16
    )
    summed = lax.psum_scatter(partial_value, "tensor", scatter_dimension=1, tiled=True).astype(
        jnp.float32
    )
    layer_out = (
        summed + adapter_scale * jnp.dot(low_bf, up_b, preferred_element_type=jnp.float32)
    ).astype(jnp.bfloat16)
    back_bf = back_total.astype(jnp.bfloat16)
    main = lax.dot_general(
        out_grad, gathered, (((1,), (1,)), ((), ())), preferred_element_type=jnp.float32
    )
    attn_grad = (
        main + adapter_scale * jnp.dot(back_bf, down_a, preferred_element_type=jnp.float32)
    ).astype(jnp.bfloat16)
    factor = adapter_scale / (attn_out.shape[0] * lax.axis_size("dp"))
    grad_a = factor * lax.dot_general(
        back_bf, attn_out, (((0,), (0,)), ((), ())), preferred_element_type=jnp.float32
    )
    grad_b = factor * lax.dot_general(
        low_bf, grad_cols, (((0,), (0,)), ((), ())), preferred_element_type=jnp.float32
    )
    bank_a, logit_grad_a = compose_back(grad_a, weights_a, picked_a, mixing_a, vector_bank)
    bank_b, logit_grad_b = compose_back(grad_b, weights_b, picked_b, mixing_b, vector_bank)
    bank_part = bank_a + bank_b
    bank_group = over_copies(bank_part, "tensor")
    bank_grad, logits_a_grad, logits_b_grad = (
        gathered_total(bank_group, "dp"),
        gathered_total(logit_grad_a, "dp"),
        gathered_total(logit_grad_b, "dp"),
    )
    return (layer_out, attn_grad, bank_grad, logits_a_grad, logits_b_grad)


def solution(mesh):
    return jax.shard_map(
        local,
        mesh=mesh,
        in_specs=(
            P("dp", "tensor"),
            P("tensor", "dp"),
            P(),
            P(None, "tensor", None),
            P(None, "tensor", None),
            P(None, "tensor", None),
            P(None, "tensor", None),
            P("dp", None),
        ),
        out_specs=(
            P("dp", "tensor"),
            P("dp", "tensor"),
            P(),
            P(None, "tensor", None),
            P(None, "tensor", None),
        ),
        check_vma=False,
    )
```

profile of v0, /device:TPU:1, one launch (start us, length us, event | category | flops | bytes accessed | tf_op | source)
XLA Modules:
  0.0 252.0 jit_solution(6651424941803468780)
XLA Ops:
  8.0 0.7 rev.7
  8.7 0.7 add_divide_fusion
  9.4 0.8 select_reduce_fusion.2
  10.2 1.2 fusion.2
  11.4 1.6 fusion.4
  13.2 0.7 rev.6
  13.9 0.7 add_divide_fusion.1
  14.6 0.8 select_reduce_fusion.3
  15.4 1.2 fusion.1
  17.6 15.2 %all_to_all.11 = f32[8,1,16384]{2,1,0:T(1,128)S(1)} all-to-all(f32[8,1,16384]{2,1,0:T(1,128)S(1)} %broadcast_in_dim.4), channel_id=1, replica_groups=mesh['dp'=16,'tensor'=8] {'tensor'}, dimensions={0} | all-to-all | bytes 1048576 | tf_op jit(solution)/shard_map/all_to_all | solution.py:11
  33.5 1.5 convolution_multiply_fusion
  36.4 30.0 %all_to_all.12 = f32[8,256,256]{2,1,0:T(8,128)S(1)} all-to-all(f32[8,256,256]{2,1,0:T(8,128)S(1)} %broadcast_in_dim.5), channel_id=1, replica_groups=mesh['dp'=16,'tensor'=8] {'tensor'}, dimensions={0} | all-to-all | bytes 4194304 | tf_op jit(solution)/shard_map/all_to_all | solution.py:11
  66.3 0.8 reduce_sum.102
  67.2 66.4 %all-gather.6.cloned.1.call-done = bf16[1024,8192]{1,0:T(8,128)(2,1)} async-done(((bf16[1024,512]{1,0:T(8,128)(2,1)}), bf16[1024,8192]{1,0:T(8,128)(2,1)}) %all-gather.6.cloned.1.call-update) | async-done | bytes 16777232 | tf_op jit(solution)/shard_map/all_gather | solution.py:63
  133.7 16.8 %convolution_convert_fusion = bf16[512,8192]{1,0:T(8,128)(2,1)} fusion(bf16[512,1024]{1,0:T(8,128)(2,1)S(1)} %copy-done, bf16[1024,8192]{1,0:T(8,128)(2,1)} %all-gather.6.cloned.1.call-done), kind=kOutput, calls=%fused_computation | convolution fusion | flops 8594128896 | bytes 26214400 | tf_op jit(solution)/shard_map/dot_general | solution.py:64
  150.5 0.9 copy-done.1
  152.1 17.9 %all-gather.1 = f32[256,4,2]{1,2,0:T(2,128)S(1)} all-gather(f32[16,4,2]{1,2,0:T(2,128)S(1)} %copy.95), channel_id=3, replica_groups=mesh['dp'=16,'tensor'=8] {'dp'}, dimensions={0}, use_global_device_ids=true | all-gather | bytes 8704 | tf_op jit(solution)/shard_map/all_gather | solution.py:28
  170.1 0.7 copy.98
  171.5 19.0 %all-gather.2 = f32[256,4,2]{1,2,0:T(2,128)S(1)} all-gather(f32[16,4,2]{1,2,0:T(2,128)S(1)} %copy.97), channel_id=4, replica_groups=mesh['dp'=16,'tensor'=8] {'dp'}, dimensions={0}, use_global_device_ids=true | all-gather | bytes 8704 | tf_op jit(solution)/shard_map/all_gather | solution.py:28
  190.6 0.7 copy.99
  191.7 3.2 %reduce_sum.103 = f32[256,256]{1,0:T(8,128)} reduce(f32[16,256,256]{2,1,0:T(8,128)} %bitcast.56, f32[]{:T(128)} %constant.5.clone.1), dimensions={0}, to_apply=%region_5.0 | reduce | flops 983040 | bytes 4456452 | tf_op jit(solution)/shard_map/reduce_sum | solution.py:29
  194.9 16.3 %add_convert_fusion = bf16[512,1024]{1,0:T(8,128)(2,1)} fusion(f32[512,1024]{1,0:T(8,128)S(1)} %fusion.23, bf16[512,8192]{1,0:T(8,128)(2,1)} %param.15, bf16[1024,8192]{1,0:T(8,128)(2,1)} %all-gather.6.cloned.1.call-done), kind=kOutput, calls=%fused_computation.1 | convolution fusion | flops 8591507456 | bytes 28311552 | tf_op jit(solution)/shard_map/dot_general | solution.py:74
  211.2 31.6 %reduce-scatter.2.cloned.1.call-done = bf16[512,1024]{1,0:T(8,128)(2,1)} async-done(((bf16[512,8192]{1,0:T(8,128)(2,1)}), bf16[512,1024]{1,0:T(8,128)(2,1)}) %reduce-scatter.2.cloned.1.call-update) | async-done | bytes 1048592 | tf_op jit(solution)/shard_map/reduce_scatter | solution.py:67
  242.9 2.6 %add_convert_fusion.1 = bf16[512,1024]{1,0:T(8,128)(2,1)} fusion(bf16[512,1024]{1,0:T(8,128)(2,1)} %reduce-scatter.2.cloned.1.call-done, bf16[512,16]{1,0:T(8,128)(2,1)S(1)} %convert_element_type.40, bf16[16,1024]{1,0:T(8,128)(2,1)S(1)} %bitcast.64), kind=kOutput, calls=%fused_computation.2 | convolution fusion | flops 18874368 | bytes 2146304 | tf_op jit(solution)/shard_map/dot_general | solution.py:71
  (51 shorter events, 5.9 us)
Async XLA Ops:
  7.2 9.5 %copy-start = (bf16[512,1024]{1,0:T(8,128)(2,1)S(1)}, bf16[512,1024]{1,0:T(8,128)(2,1)}, u32[]{:S(2)}) copy-start(bf16[512,1024]{1,0:T(8,128)(2,1)} %param.8) | copy-start | bytes 3145732
  7.2 126.5 %all-gather.6.cloned.1.call-start = ((), (), s32[]{:S(2)}) async-start(), calls=%async_computation.3 | async-start | bytes 17825792 | tf_op jit(solution)/shard_map/all_gather | solution.py:63
  7.9 183.8 %all-gather.8.cloned.1.call-start = ((), (), s32[]{:S(2)}) async-start(), calls=%async_computation.5 | async-start | bytes 4456448 | tf_op jit(solution)/shard_map/all_gather | solution.py:28
  11.4 21.9 %copy-start.2 = (bf16[4,2,8,256]{3,2,0,1:T(8,128)(2,1)}, bf16[4,2,8,256]{3,2,0,1:T(8,128)(2,1)S(1)}, u32[]{:S(2)}) copy-start(bf16[4,2,8,256]{3,2,0,1:T(8,128)(2,1)S(1)} %copy.105) | copy-start | bytes 98308
  16.6 16.6 %copy-start.4 = (bf16[4,2,8,256]{3,2,0,1:T(8,128)(2,1)}, bf16[4,2,8,256]{3,2,0,1:T(8,128)(2,1)S(1)}, u32[]{:S(2)}) copy-start(bf16[4,2,8,256]{3,2,0,1:T(8,128)(2,1)S(1)} %copy.104) | copy-start | bytes 98308
  67.2 175.7 %reduce-scatter.2.cloned.1.call-start = ((), (), s32[]{:S(2)}) async-start(), calls=%async_computation.4 | async-start | bytes 9437184 | tf_op jit(solution)/shard_map/reduce_scatter | solution.py:67
  150.5 0.9 copy-start.1
  150.5 1.3 copy-start.6
  150.5 20.7 %copy-start.7 = (s32[16,4,2]{0,2,1:T(2,128)S(1)}, s32[16,4,2]{0,2,1:T(2,128)}, u32[]{:S(2)}) copy-start(s32[16,4,2]{0,2,1:T(2,128)} %param.14) | copy-start | bytes 1540
  150.5 40.8 %copy-start.5 = (bf16[4,2,8,256]{3,2,0,1:T(8,128)(2,1)S(1)}, bf16[4,2,8,256]{3,2,0,1:T(8,128)(2,1)}, u32[]{:S(2)}) copy-start(bf16[4,2,8,256]{3,2,0,1:T(8,128)(2,1)} %copy-done.4) | copy-start | bytes 98308
  194.9 48.0 %copy-start.3 = (bf16[4,2,8,256]{3,2,0,1:T(8,128)(2,1)S(1)}, bf16[4,2,8,256]{3,2,0,1:T(8,128)(2,1)}, u32[]{:S(2)}) copy-start(bf16[4,2,8,256]{3,2,0,1:T(8,128)(2,1)} %copy-done.2) | copy-start | bytes 98308
Sparse Core Ops, SparseCore 0:
  10.1 123.4 all-gather.5
  136.4 52.7 all-gather.7
  191.5 51.2 reduce-scatter.1
where the time goes:
time: 253 us; the launch traced here: 252 us
  waiting for transfers between devices  98.8 us (39%)
  blocking collectives  82 us (32%)
  matrix products  43.9 us (17%)
  between operations  14 us (6%)
  other arithmetic  8.13 us (3%)
  local copies, waits for them, and re-layouts  5.05 us (2%)
    all_gather x1, waiting for transfers between devices, local(): gathered = lax.all_gather(frozen_weight, 'dp', axis=1, tiled=True)  66.4 us
    all_to_all x2, blocking collectives, from_everyone(): return lax.all_to_all(copies, axis, split_axis=0, concat_axis=0, tiled=True)  45.1 us
    all_gather x2, blocking collectives, gathered_total(): parts = lax.all_gather(x, axis)  36.9 us
    reduce_scatter x1, waiting for transfers between devices, local(): lax.psum_scatter(partial_value, 'tensor', scatter_dimension=1, tiled=True)  31.6 us
    dot_general x1, matrix products, local(): jnp.dot(attn_out, gathered, preferred_element_type=jnp.float32)  16.8 us
    dot_general x1, matrix products, local(): lax.dot_general(out_grad, gathered, (((1,), (1,)), ((), ())), preferred_e...  16.3 us
  transfers between devices with their start and end apart: 3, of which 2 were waited for; matrix products, arithmetic and copies ran while one was open for 21% of the time, Pallas kernels for 0%

commit v1 on v0

--- a/solution.py
+++ b/solution.py
@@ -1,9 +1,25 @@
+import functools
 import jax
 import jax.numpy as jnp
 from jax import lax
 from jax.sharding import PartitionSpec as P
 
 adapter_scale = 2.0
+
+
+def save_files(page, axis_k):
+    return jnp.concatenate(
+        lax.all_to_all(
+            jnp.stack([page for _ in range(lax.axis_size("dp"))], axis=0),
+            axis_name="dp",
+            split_axis=0,
+            concat_axis=0,
+        ),
+        axis=axis_k,
+    )
+
+
+_convert_numbers = functools.partial(save_files, axis_k=1)
 
 
 def from_everyone(x, axis):
@@ -60,7 +76,7 @@
     back_part = jnp.dot(grad_cols, up_b.T, preferred_element_type=jnp.float32)
     low_total, back_total = packed_total((low_part, back_part), "tensor")
     low_bf = low_total.astype(jnp.bfloat16)
-    gathered = lax.all_gather(frozen_weight, "dp", axis=1, tiled=True)
+    gathered = _convert_numbers(frozen_weight)
     partial_value = jnp.dot(attn_out, gathered, preferred_element_type=jnp.float32).astype(
         jnp.bfloat16
     )

time: 253 us -> 495 us (1.96)
  the two profiles are of different devices: /device:TPU:1 before, /device:TPU:18 now
where the time goes in v1:
time: 495 us; the launch traced here: 494 us
  waiting for transfers between devices  258 us (52%)
  blocking collectives  125 us (25%)
  matrix products  56 us (11%)
  between operations  15.7 us (3%)
  local copies, waits for them, and re-layouts  15.6 us (3%)
  starting transfers between devices  15.1 us (3%)
  other arithmetic  8.23 us (2%)
    all_to_all x1, waiting for transfers between devices, save_files(): lax.all_to_all(jnp.stack([page for _ in range(lax.axis_size('dp'))], axis...  236 us
    all_gather x2, blocking collectives, gathered_total(): parts = lax.all_gather(x, axis)  114 us
    dot_general x1, matrix products, local(): jnp.dot(attn_out, gathered, preferred_element_type=jnp.float32)  29.6 us
    all_to_all x1, waiting for transfers between devices, from_everyone(): return lax.all_to_all(copies, axis, split_axis=0, concat_axis=0, tiled=True)  21.8 us
    dot_general x1, matrix products, local(): lax.dot_general(out_grad, gathered, (((1,), (1,)), ((), ())), preferred_e...  15.6 us
    all_to_all x1, blocking collectives, from_everyone(): return lax.all_to_all(copies, axis, split_axis=0, concat_axis=0, tiled=True)  11.8 us
  transfers between devices with their start and end apart: 4, of which 2 were waited for; matrix products, arithmetic and copies ran while one was open for 11% of the time, Pallas kernels for 0%

profile of v1, /device:TPU:18, one launch (start us, length us, event | category | flops | bytes accessed | tf_op | source)
XLA Modules:
  0.0 494.2 jit_solution(12415607691547703877)
XLA Ops:
  8.0 0.8 rev.7
  9.5 0.8 select_reduce_fusion.2
  10.3 1.2 fusion.2
  11.6 1.6 fusion.4
  13.3 0.7 rev.6
  14.7 0.8 select_reduce_fusion.3
  15.5 1.2 fusion.1
  17.8 11.8 %all_to_all.16 = f32[8,1,16384]{2,1,0:T(1,128)S(1)} all-to-all(f32[8,1,16384]{2,1,0:T(1,128)S(1)} %broadcast_in_dim.4), channel_id=1, replica_groups=mesh['dp'=16,'tensor'=8] {'tensor'}, dimensions={0} | all-to-all | bytes 1048576 | tf_op jit(solution)/shard_map/all_to_all | solution.py:27
  30.3 1.5 convolution_multiply_fusion
  33.0 1.5 broadcast_in_dim.5
  34.5 6.7 %all-to-all-start.2 = ((f32[8,256,256]{2,1,0:T(8,128)}), f32[8,256,256]{2,1,0:T(8,128)S(1)}, u32[]{:S(2)}, u32[]{:S(2)}) async-start(f32[8,256,256]{2,1,0:T(8,128)} %broadcast_in_dim.5), calls=%async_computation.3 | async-start | bytes 4194304 | tf_op jit(solution)/shard_map/all_to_all | solution.py:27
  41.2 2.3 copy.91
  43.5 21.8 %all-to-all-done.2 = f32[8,256,256]{2,1,0:T(8,128)S(1)} async-done(((f32[8,256,256]{2,1,0:T(8,128)}), f32[8,256,256]{2,1,0:T(8,128)S(1)}, u32[]{:S(2)}, u32[]{:S(2)}) %all-to-all-start.2) | async-done | bytes 2097184 | tf_op jit(solution)/shard_map/all_to_all | solution.py:27
  65.2 6.9 %stack.2 = bf16[16,1024,512]{1,2,0:T(8,128)(2,1)} broadcast(bf16[1024,512]{0,1:T(8,128)(2,1)} %copy.91), dimensions={1,2} | broadcast | bytes 17825792 | tf_op jit(solution)/shard_map/stack | solution.py:13
  72.1 8.3 %all-to-all-start = ((bf16[16,1024,512]{1,2,0:T(8,128)(2,1)}), bf16[16,1024,512]{1,2,0:T(8,128)(2,1)}, u32[]{:S(2)}, u32[]{:S(2)}) async-start(bf16[16,1024,512]{1,2,0:T(8,128)(2,1)} %stack.2), calls=%async_computation | async-start | bytes 33554432 | tf_op jit(solution)/shard_map/all_to_all | solution.py:12
  80.4 0.8 reduce_sum.102
  81.4 236.4 %all-to-all-done = bf16[16,1024,512]{1,2,0:T(8,128)(2,1)} async-done(((bf16[16,1024,512]{1,2,0:T(8,128)(2,1)}), bf16[16,1024,512]{1,2,0:T(8,128)(2,1)}, u32[]{:S(2)}, u32[]{:S(2)}) %all-to-all-start) | async-done | bytes 16777248 | tf_op jit(solution)/shard_map/all_to_all | solution.py:12
  317.7 29.6 %convolution_convert_fusion = bf16[512,8192]{1,0:T(8,128)(2,1)} fusion(bf16[512,1024]{1,0:T(8,128)(2,1)S(1)} %copy-done, bf16[1024,8192]{0,1:T(8,128)(2,1)} %bitcast.1), kind=kOutput, calls=%fused_computation | convolution fusion | flops 8594128896 | bytes 26214400 | tf_op jit(solution)/shard_map/dot_general | solution.py:80
  347.4 0.9 copy-done.2
  349.0 89.4 %all-gather.1 = f32[256,4,2]{1,2,0:T(2,128)S(1)} all-gather(f32[16,4,2]{1,2,0:T(2,128)S(1)} %copy.100), channel_id=3, replica_groups=mesh['dp'=16,'tensor'=8] {'dp'}, dimensions={0}, use_global_device_ids=true | all-gather | bytes 8704 | tf_op jit(solution)/shard_map/all_gather | solution.py:44
  439.9 24.1 %all-gather.2 = f32[256,4,2]{1,2,0:T(2,128)S(1)} all-gather(f32[16,4,2]{1,2,0:T(2,128)S(1)} %copy.102), channel_id=4, replica_groups=mesh['dp'=16,'tensor'=8] {'dp'}, dimensions={0}, use_global_device_ids=true | all-gather | bytes 8704 | tf_op jit(solution)/shard_map/all_gather | solution.py:44
  465.2 3.3 reduce_sum.103
  468.5 15.6 %add_convert_fusion = bf16[512,1024]{1,0:T(8,128)(2,1)} fusion(f32[512,1024]{1,0:T(8,128)S(1)} %fusion.23, bf16[512,8192]{1,0:T(8,128)(2,1)} %param.15, bf16[1024,8192]{0,1:T(8,128)(2,1)} %bitcast.1), kind=kOutput, calls=%fused_computation.1 | convolution fusion | flops 8591507456 | bytes 28311552 | tf_op jit(solution)/shard_map/dot_general | solution.py:90
  484.2 2.6 add_convert_fusion.1
  (55 shorter events, 7.8 us)
Async XLA Ops:
  8.0 8.8 %copy-start = (bf16[512,1024]{1,0:T(8,128)(2,1)S(1)}, bf16[512,1024]{1,0:T(8,128)(2,1)}, u32[]{:S(2)}) copy-start(bf16[512,1024]{1,0:T(8,128)(2,1)} %param.8) | copy-start | bytes 3145732
  11.5 5.9 %copy-start.3 = (bf16[4,2,8,256]{3,2,0,1:T(8,128)(2,1)}, bf16[4,2,8,256]{3,2,0,1:T(8,128)(2,1)S(1)}, u32[]{:S(2)}) copy-start(bf16[4,2,8,256]{3,2,0,1:T(8,128)(2,1)S(1)} %copy.110) | copy-start | bytes 98308
  16.8 0.7 copy-start.5
  34.5 30.7 %all-to-all-start.2 = ((f32[8,256,256]{2,1,0:T(8,128)}), f32[8,256,256]{2,1,0:T(8,128)S(1)}, u32[]{:S(2)}, u32[]{:S(2)}) async-start(f32[8,256,256]{2,1,0:T(8,128)} %broadcast_in_dim.5), calls=%async_computation.3 | async-start | bytes 4194304 | tf_op jit(solution)/shard_map/all_to_all | solution.py:27
  72.1 245.6 %all-to-all-start = ((bf16[16,1024,512]{1,2,0:T(8,128)(2,1)}), bf16[16,1024,512]{1,2,0:T(8,128)(2,1)}, u32[]{:S(2)}, u32[]{:S(2)}) async-start(bf16[16,1024,512]{1,2,0:T(8,128)(2,1)} %stack.2), calls=%async_computation | async-start | bytes 33554432 | tf_op jit(solution)/shard_map/all_to_all | solution.py:12
  80.4 384.9 %all-gather.5.cloned.1.call-start = ((), (), s32[]{:S(2)}) async-start(), calls=%async_computation.5 | async-start | bytes 4456448 | tf_op jit(solution)/shard_map/all_gather | solution.py:44
  81.3 402.9 %reduce-scatter.2.cloned.1.call-start = ((), (), s32[]{:S(2)}) async-start(), calls=%async_computation.4 | async-start | bytes 9437184 | tf_op jit(solution)/shard_map/reduce_scatter | solution.py:83
  347.3 0.9 copy-start.2
  347.3 1.3 copy-start.7
  347.3 92.2 %copy-start.8 = (s32[16,4,2]{0,2,1:T(2,128)S(1)}, s32[16,4,2]{0,2,1:T(2,128)}, u32[]{:S(2)}) copy-start(s32[16,4,2]{0,2,1:T(2,128)} %param.14) | copy-start | bytes 1540
  347.3 117.5 %copy-start.6 = (bf16[4,2,8,256]{3,2,0,1:T(8,128)(2,1)S(1)}, bf16[4,2,8,256]{3,2,0,1:T(8,128)(2,1)}, u32[]{:S(2)}) copy-start(bf16[4,2,8,256]{3,2,0,1:T(8,128)(2,1)} %copy-done.5) | copy-start | bytes 98308
  468.5 15.6 %copy-start.4 = (bf16[4,2,8,256]{3,2,0,1:T(8,128)(2,1)S(1)}, bf16[4,2,8,256]{3,2,0,1:T(8,128)(2,1)}, u32[]{:S(2)}) copy-start(bf16[4,2,8,256]{3,2,0,1:T(8,128)(2,1)} %copy-done.3) | copy-start | bytes 98308
  468.5 18.3 %copy-start.1 = (bf16[512,1024]{1,0:T(8,128)(2,1)S(1)}, bf16[512,1024]{1,0:T(8,128)(2,1)}, u32[]{:S(2)}) copy-start(bf16[512,1024]{1,0:T(8,128)(2,1)} %param.8) | copy-start | bytes 3145732
Sparse Core Ops, SparseCore 0:
  83.9 243.9 all-gather.4
Sparse Core Ops, SparseCore 1:
  347.5 118.7 reduce-scatter.1
